TPU v7x, 32 devices: a whole 2x2x4 slice. The times are simulated.
32 devices in a mesh: ctx: 8 (over z, x), col: 4 (over y, core).
Axes of the slice: x: 2, y: 2, z: 4, core: 2. Of those that a mesh axis runs over, the one named last changes fastest.
Arguments:
- sequence: bfloat16 [4096, 4096], P('ctx', 'col'), may hold values from -6 to 6
- w_proj: bfloat16 [4096, 3, 2048], P('col'), may hold values from -0.125 to 0.125
- short_filter: float32 [3, 3, 2048], P(None, None, 'col'), may hold values from -3 to 3
- long_filter: float32 [4096, 2048], P('ctx', 'col'), may hold values from -0.09375 to 0.09375
- skip_gain: float32 [2048], P('col'), may hold values from 0.5 to 1.5
Outputs:
- mixed: float32 [4096, 2048], P('ctx', 'col')
All inputs are finite; a program needn't handle non-finite values.
Results may differ from a plain program's by a relative error of at most 0.0003.
Values sent between devices are 32-bit elements; how exact they have to be, the bound alone decides.
No kernel may reach another device: no remote copies, remote signals or barrier semaphores. Data moves between devices by JAX's collectives and lax.ppermute only.
A program may use at most 128 MiB of HBM per device.

v0:
```python
import functools
import math

import jax
import jax.numpy as jnp
import numpy as np
from jax import lax
from jax.experimental import pallas as pl
from jax.experimental.pallas import tpu as pltpu
from jax.sharding import PartitionSpec as P


LANES = 128
SUBLANES = 8

KERNEL_VMEM = 12 * 2**20
PROJECT_VMEM = 53 * 2**20
VMEM_SPEC = pl.BlockSpec(memory_space=pltpu.VMEM)


def turned(pair, count, length):
    real, imag = pair
    c = math.cos(2.0 * math.pi * count / length)
    s = math.sin(2.0 * math.pi * count / length)
    return (real * c + imag * s, imag * c - real * s)


def real_forward(blocks):
    count = len(blocks)
    if count == 2:
        return [(blocks[0] + blocks[1], None), (blocks[0] - blocks[1], None)]
    half, quarter = count // 2, count // 4
    even, odd = real_forward(blocks[0::2]), real_forward(blocks[1::2])
    terms = [None] * (half + 1)
    for k in range(quarter + 1):
        even_real, even_imag = even[k]
        if k == 0:
            terms[0] = (even_real + odd[0][0], None)
            terms[half] = (even_real - odd[0][0], None)
        elif k == quarter:
            terms[k] = (even_real, -odd[k][0])
        else:
            odd_real, odd_imag = turned(odd[k], k, count)
            terms[k] = (even_real + odd_real, even_imag + odd_imag)
            terms[half - k] = (even_real - odd_real, odd_imag - even_imag)
    return terms


def real_inverse(terms):
    half = len(terms) - 1
    count = 2 * half
    if count == 2:
        return [terms[0][0] + terms[1][0], terms[0][0] - terms[1][0]]
    quarter = half // 2
    even, odd = [], []
    for k in range(quarter + 1):
        (a_real, a_imag), (b_real, b_imag) = terms[k], terms[half - k]
        if k == 0:
            even.append((a_real + b_real, None))
            odd.append((a_real - b_real, None))
        elif k == quarter:
            even.append((2.0 * a_real, None))
            odd.append((-2.0 * a_imag, None))
        else:
            even.append((a_real + b_real, a_imag - b_imag))
            odd.append(turned((a_real - b_real, a_imag + b_imag), -k, count))
    result = [None] * count
    result[0::2] = real_inverse(even)
    result[1::2] = real_inverse(odd)
    return result


def split_table(table):
    table = jnp.asarray(table, jnp.float32)
    high = table.astype(jnp.bfloat16)
    return jnp.stack([high, (table - high.astype(jnp.float32)).astype(jnp.bfloat16)])


def tables(blocks):
    step = np.arange(LANES)
    angle = 2.0 * np.pi / LANES * (step[:, None] * step[None, :] % LANES)
    c, s = np.cos(angle), np.sin(angle)
    forward = np.block([[c, -s], [s, c]])
    total = blocks * LANES
    turn = 2.0 * np.pi / total * (np.arange(blocks // 2 + 1)[:, None] * step[None, :])
    turns = np.stack([np.cos(turn), np.sin(turn)])[:, :, None, :]
    return (
        split_table(forward),
        split_table(forward.T),
        jnp.asarray(turns, jnp.float32),
    )


def split_dot(left, table_ref):
    high = left.astype(jnp.bfloat16)
    low = (left - high.astype(jnp.float32)).astype(jnp.bfloat16)
    dot = functools.partial(jnp.dot, preferred_element_type=jnp.float32)
    return dot(high, table_ref[0]) + (dot(low, table_ref[0]) + dot(high, table_ref[1]))


def lane_blocks(ref, rows):
    sources, _, width = ref.shape
    return [
        ref[p, rows, i * LANES : (i + 1) * LANES]
        for p in range(sources)
        for i in range(width // LANES)
    ]


def forward_rows(in_ref, stage_ref, turns_ref):
    channels = in_ref.shape[1]

    def group(g, carry):
        rows = pl.ds(pl.multiple_of(g * SUBLANES, SUBLANES), SUBLANES)
        for k, (real, imag) in enumerate(real_forward(lane_blocks(in_ref, rows))):
            c, s = turns_ref[0, k], turns_ref[1, k]
            if imag is None:
                stage_ref[k, rows, :LANES] = real * c
                stage_ref[k, rows, LANES:] = -(real * s)
            else:
                stage_ref[k, rows, :LANES] = real * c + imag * s
                stage_ref[k, rows, LANES:] = imag * c - real * s
        return carry

    lax.fori_loop(0, channels // SUBLANES, group, 0)


def convolve_kernel(
    in_ref, spectrum_ref, forward_ref, inverse_ref, turns_ref, out_ref, stage_ref
):
    terms, channels, width = stage_ref.shape
    forward_rows(in_ref, stage_ref, turns_ref)
    rows = stage_ref[...].reshape(terms * channels, width)
    signal = split_dot(rows, forward_ref)
    other = spectrum_ref[...].reshape(terms * channels, width)
    s_real, s_imag = signal[:, :LANES], signal[:, LANES:]
    f_real, f_imag = other[:, :LANES], other[:, LANES:]
    product = jnp.concatenate(
        [s_real * f_real - s_imag * f_imag, s_real * f_imag + s_imag * f_real], axis=1
    )
    stage_ref[...] = split_dot(product, inverse_ref).reshape(terms, channels, width)
    _, _, tokens = in_ref.shape
    per_source = tokens // LANES

    def group(g, carry):
        group_rows = pl.ds(pl.multiple_of(g * SUBLANES, SUBLANES), SUBLANES)
        pairs = []
        for k in range(terms):
            real = stage_ref[k, group_rows, :LANES]
            imag = stage_ref[k, group_rows, LANES:]
            c, s = turns_ref[0, k], turns_ref[1, k]
            pairs.append((real * c - imag * s, imag * c + real * s))
        for m, block in enumerate(real_inverse(pairs)):
            i = m % per_source
            out_ref[m // per_source, group_rows, i * LANES : (i + 1) * LANES] = block
        return carry

    lax.fori_loop(0, channels // SUBLANES, group, 0)


def stage_shape(shape):
    sources, channels, tokens = shape
    return (sources * tokens // LANES // 2 + 1, channels, 2 * LANES)


def call(kernel, out_shape, operands, scratch=(), after=(), scalar=None, hbm=(), vmem=KERNEL_VMEM):
    wrapped = kernel
    n_scalar, n_in = int(scalar is not None), len(operands) + len(hbm)
    if after:

        def wrapped(*refs):
            return kernel(*refs[: n_scalar + n_in], *refs[n_scalar + n_in + len(after) :])

    anywhere = pl.BlockSpec(memory_space=pl.ANY)
    stays = pl.BlockSpec(memory_space=pltpu.HBM)
    specs = [VMEM_SPEC] * len(operands) + [stays] * len(hbm) + [anywhere] * len(after)
    lead = ()
    if scalar is not None:
        specs, lead = [pl.BlockSpec(memory_space=pltpu.SMEM)] + specs, (scalar,)
    return pl.pallas_call(
        wrapped,
        out_shape=out_shape,
        in_specs=specs,
        out_specs=jax.tree.map(lambda _: VMEM_SPEC, out_shape),
        scratch_shapes=list(scratch),
        compiler_params=pltpu.CompilerParams(vmem_limit_bytes=vmem),
    )(*lead, *operands, *hbm, *after)


def f32(*shape):
    return jax.ShapeDtypeStruct(shape, jnp.float32)


def spectrum_kernel(scale, offsets, in_ref, table_ref, turns_ref, *refs):
    out_refs, stage_ref = refs[:-1], refs[-1]
    terms, _, width = stage_ref.shape
    forward_rows(in_ref, stage_ref, turns_ref)
    for out_ref, first in zip(out_refs, offsets):
        count = out_ref.shape[1]
        rows = stage_ref[:, first : first + count, :].reshape(terms * count, width)
        out_ref[...] = (split_dot(rows, table_ref) * scale).reshape(terms, count, width)


def spectrum(received, forward, turns, chunks, after):
    owners, channels, tokens = received.shape
    terms, _, width = stage_shape(received.shape)
    return call(
        functools.partial(
            spectrum_kernel, 1.0 / (owners * tokens), [start // owners for start, _ in chunks]
        ),
        [f32(terms, size // owners, width) for _, size in chunks],
        (received, forward, turns),
        scratch=[pltpu.VMEM((terms, channels, width), jnp.float32)],
        after=after,
    )


def convolve_apart_kernel(me_ref, *refs):
    ins, outs, (stage_ref, whole_ref) = refs[:5], refs[5:-2], refs[-2:]
    convolve_kernel(*ins, whole_ref, stage_ref)
    for k, out_ref in enumerate(outs):
        out_ref[...] = whole_ref[me_ref[0] ^ k]


def convolve(received, filter_spectrum, forward, inverse, turns, me=None, after=()):
    operands = (received, filter_spectrum, forward, inverse, turns)
    stage = pltpu.VMEM(stage_shape(received.shape), jnp.float32)
    if me is None:
        return call(convolve_kernel, f32(*received.shape), operands, (stage,), after)
    return call(
        convolve_apart_kernel,
        [f32(*received.shape[1:])] * received.shape[0],
        operands,
        (stage, pltpu.VMEM(received.shape, jnp.float32)),
        after,
        me,
    )


def project_kernel(tasks, owner_width, load_rows, owner_ref, *refs):
    if load_rows:
        x_hbm, w_ref = refs[:2]
        outs, (x_ref, held_ref, sems) = refs[2:-3], refs[-3:]
        rows_copy = pltpu.make_async_copy(x_hbm, x_ref, sems.at[len(tasks)])
        rows_copy.start()
    else:
        x_ref, w_ref = refs[:2]
        outs, (held_ref, sems) = refs[2:-2], refs[-2:]

    def copy(index):
        _, _, which, _, j, start, size = tasks[index]
        at = pl.multiple_of(owner_ref[which] * owner_width + start, LANES)
        return pltpu.make_async_copy(
            w_ref.at[j, :, pl.ds(at, size)],
            held_ref.at[index, :, pl.ds(0, size)],
            sems.at[index],
        )

    for index in range(len(tasks)):
        copy(index).start()
    if load_rows:
        rows_copy.wait()
    for index, (output, slot, _, rows, _, _, size) in enumerate(tasks):
        copy(index).wait()
        outs[output][slot] = jnp.dot(
            x_ref[0:rows], held_ref[index, :, 0:size], preferred_element_type=jnp.float32
        )


def project(rows, weight, owners, owner_width, pieces, after=(), load_rows=False):
    depth = weight.shape[1]
    tasks = tuple(
        (output, slot, which, count, j, start, size)
        for output, (which, count, js, start, size) in enumerate(pieces)
        for slot, j in enumerate(js)
    )
    widest = max(size for *_, size in pieces)
    scratch = [
        pltpu.VMEM((len(tasks), depth, widest), weight.dtype),
        pltpu.SemaphoreType.DMA((len(tasks) + 1,)),
    ]
    if load_rows:
        scratch = [pltpu.VMEM(rows.shape, rows.dtype)] + scratch
    return call(
        functools.partial(project_kernel, tasks, owner_width, load_rows),
        [f32(len(js), count, size) for _, count, js, _, size in pieces],
        () if load_rows else (rows,),
        scratch=scratch,
        after=after,
        scalar=owners,
        hbm=(rows, weight) if load_rows else (weight,),
        vmem=PROJECT_VMEM,
    )


def last_rows_kernel(x_ref, out_ref):
    out_ref[...] = x_ref[...].astype(jnp.float32)


def extend_kernel(rim_ref, x_ref, out_ref):
    lead = rim_ref.shape[0]
    out_ref[0:lead] = rim_ref[...].astype(out_ref.dtype)
    out_ref[lead:] = x_ref[...]


def short_filtered(tap_ref, j, ext_ref, slot, start, size):
    taken = lambda back: ext_ref[slot, pl.ds(SUBLANES + start - back, size), :]
    return (
        tap_ref[0, j : j + 1, :] * taken(0)
        + tap_ref[1, j : j + 1, :] * taken(1)
        + tap_ref[2, j : j + 1, :] * taken(2)
    )


def fill_extended(ext_ref, slot, cols, refs):
    near, core, far = refs[0], refs[1], refs[2:]
    if len(far) == 1:
        ext_ref[slot] = near[slot, :, cols] + core[slot, :, cols] + far[0][slot, :, cols]
        return
    for rows, ref in ((slice(0, SUBLANES), far[0]), (slice(SUBLANES, None), far[1])):
        ext_ref[slot, rows, :] = (
            near[slot, rows, cols] + core[slot, rows, cols] + ref[slot, :, cols]
        )


def gate_kernel(offset, *refs):
    parts, (tap_ref, out_ref, ext_ref) = refs[:-3], refs[-3:]
    width = parts[0].shape[2]
    _, channels, tokens = out_ref.shape
    for at in range(0, width, LANES):
        cols = slice(at, at + LANES)
        taps = tap_ref.at[:, :, offset + at : offset + at + LANES]
        for slot in range(2):
            fill_extended(ext_ref, slot, cols, parts)
        for start in range(0, tokens, LANES):
            key = short_filtered(taps, 1, ext_ref, 0, start, LANES)
            value = short_filtered(taps, 2, ext_ref, 1, start, LANES)
            block = (key * value).T
            for piece in range(LANES // channels):
                out_ref[at // channels + piece, :, start : start + LANES] = block[
                    piece * channels : (piece + 1) * channels
                ]


def gate(parts, taps, start, owners, after=()):
    _, rows, width = parts[0].shape
    return call(
        functools.partial(gate_kernel, start),
        f32(owners, width // owners, rows - SUBLANES),
        (*parts, taps),
        scratch=[pltpu.VMEM((2, rows, LANES), jnp.float32)],
        after=after,
    )


def pack_kernel(chunks, first_ref, filter_ref, skip_ref, out_ref):
    tokens = filter_ref.shape[0]
    owners = out_ref.shape[0]
    for at in range(0, filter_ref.shape[1], LANES):
        start, width = next(c for c in chunks if c[0] <= at < c[0] + c[1])
        channels = width // owners
        for row in range(0, tokens, LANES):
            block = filter_ref[row : row + LANES, at : at + LANES]
            if row == 0:
                added = skip_ref[:, at : at + LANES] * first_ref[0].astype(jnp.float32)
                top = lax.broadcasted_iota(jnp.int32, block.shape, 0) == 0
                block = jnp.where(top, block + added, block)
            block = block.T
            for piece in range(LANES // channels):
                owner = (at - start) // channels + piece
                out_ref[
                    owner, start // owners : start // owners + channels, row : row + LANES
                ] = block[piece * channels : (piece + 1) * channels]


def end_kernel(chunks, apart, me_ref, *refs):
    n = len(chunks)
    owners = refs[0].shape[0] if not apart else apart
    count = n - 1 + owners if apart else n
    parts, (tap_ref, out_ref, ext_ref, whole_ref) = refs[count:-4], refs[-4:]
    tokens, _ = out_ref.shape
    blocks = list(refs[:n])
    if apart:
        for k in range(owners):
            whole_ref[me_ref[0] ^ k] = refs[k][...]
        blocks = [whole_ref] + list(refs[owners:count])
    for ref, (start, width) in zip(blocks, chunks):
        channels = ref.shape[1]
        for at in range(start, start + width, LANES):
            cols = slice(at, at + LANES)
            fill_extended(ext_ref, 0, cols, parts)
            taps = tap_ref.at[:, :, cols]
            held = LANES // channels
            first = (at - start) // channels
            for row in range(0, tokens, LANES):
                query = short_filtered(taps, 0, ext_ref, 0, row, LANES)
                block = ref[first : first + held, :, row : row + LANES].reshape(LANES, LANES)
                out_ref[row : row + LANES, cols] = query * block.T


def chunk_list(width, owners):
    grain = max(LANES, SUBLANES * owners)
    size = max(grain, width // 2)
    return tuple((start, size) for start in range(0, width, size))


def exchanged(block, axis, stride):
    size = lax.axis_size(axis)
    return lax.ppermute(block, axis, [(i, i ^ stride) for i in range(size)])


def on_device(sequence, w_proj, short_filter, long_filter, skip_gain):
    tokens, depth = sequence.shape
    width = long_filter.shape[1]
    owners = lax.axis_size("ctx")
    chunks = chunk_list(width, owners)
    weight = w_proj.transpose(1, 0, 2)
    col = lax.axis_index("col")
    owner = jnp.stack([col ^ d for d in range(4)]).astype(jnp.int32)
    forward, inverse, turns = tables(owners * tokens // LANES)
    rows = tokens + SUBLANES
    both = (1, 2)

    def turn_over(block):
        return lax.all_to_all(block, "ctx", 0, 0, tiled=True)

    def swap(block, stride):
        return exchanged(block, "col", stride)

    start, size = chunks[0]
    sent, kept = project(
        sequence,
        weight,
        owner,
        width,
        [(3, tokens, both, start, size), (2, tokens, both, start, size)],
        load_rows=True,
    )
    first_far = kept + swap(sent, 1)
    first_body = swap(first_far, 2)

    rim = call(
        last_rows_kernel, f32(SUBLANES, depth), (sequence[tokens - SUBLANES :],), after=(first_far,)
    )
    rim_got = lax.ppermute(rim, "ctx", [(i, (i + 1) % owners) for i in range(owners)])
    packed = call(
        functools.partial(pack_kernel, chunks),
        f32(owners, width // owners, tokens),
        (long_filter, skip_gain[None]),
        after=(rim,),
        scalar=(lax.axis_index("ctx") == 0)[None].astype(jnp.int32),
    )
    filter_got = turn_over(packed)
    extended = call(
        extend_kernel,
        jax.ShapeDtypeStruct((rows, depth), sequence.dtype),
        (rim_got, sequence),
        after=(packed,),
    )

    def pieces(far, near):
        listed = [(far, SUBLANES, both, start, size)]
        listed += [(far, rows, both, start, size) for start, size in chunks[1:]]
        return listed + [(far, rows, (0,), 0, width), (near, rows, both, start, size)]

    sent = project(extended, weight, owner, width, pieces(3, 1))
    kept = project(extended, weight, owner, width, pieces(2, 0), after=sent[:1])
    got = [swap(s, 1) for s in sent]
    far_sums = [k + g for k, g in zip(kept[:-1], got)]
    far = [swap(s, 2) for s in far_sums]
    far_parts = [(far[0], first_body)] + [(f,) for f in far[1:]]
    parts = [(kept[-1], got[-1])]

    def gated_chunk(index, after):
        part = (*parts[index], *far_parts[index])
        return gate(part, short_filter, chunks[index][0], owners, after)

    gated = gated_chunk(0, tuple(far_sums))

    def pieces(near):
        listed = [(near, rows, both, start, size) for start, size in chunks[1:]]
        return listed + [(near, rows, (0,), 0, width)]

    sent = project(extended, weight, owner, width, pieces(1), after=(gated,))
    kept = project(extended, weight, owner, width, pieces(0), after=sent[:1])
    parts += [(k, swap(s, 1)) for k, s in zip(kept, sent)]
    spectra = spectrum(filter_got, forward, turns, chunks, tuple(kept[:1]))
    last = len(chunks) - 1
    me = lax.axis_index("ctx")[None].astype(jnp.int32)
    convolved, done = [], spectra[0]
    for index in range(len(chunks)):
        arrived = turn_over(gated)
        apart = index == 0 < last
        done = convolve(
            arrived, spectra[index], forward, inverse, turns, me if apart else None
        )
        if index < last:
            gated = gated_chunk(index + 1, tuple(done[:1]) if apart else (done,))
        if apart:
            convolved.append(done[0])
            for k in range(1, owners):
                convolved.append(exchanged(done[k], "ctx", k))
        else:
            convolved.append(turn_over(done))
    return call(
        functools.partial(end_kernel, chunks, owners if last else 0),
        f32(tokens, width),
        (*convolved, *parts[-1], *far_parts[-1], short_filter),
        scratch=[
            pltpu.VMEM((1, rows, LANES), jnp.float32),
            pltpu.VMEM((owners, chunks[0][1] // owners, tokens), jnp.float32),
        ],
        scalar=me,
    )


def solution(mesh):
    return jax.shard_map(
        on_device,
        mesh=mesh,
        in_specs=(
            P("ctx", "col"),
            P("col", None, None),
            P(None, None, "col"),
            P("ctx", "col"),
            P("col"),
        ),
        out_specs=P("ctx", "col"),
        check_vma=False,
    )
```

profile of v0, /device:TPU:0, one launch (start us, length us, event | category | flops | bytes accessed | tf_op | source)
XLA Modules:
  0.0 175.5 jit_solution(2945371431096628934)
XLA Ops:
  0.1 5.7 %shard_map.82 = (f32[2,512,256]{2,1,0:T(8,128)}, f32[2,512,256]{2,1,0:T(8,128)}) custom-call(s32[4]{0:T(128)S(1)} %pad_add_fusion.owner_ref.refs_0_, bf16[512,1024]{1,0:T(8,128)(2,1)} %refs_1_.3, bf16[3,1024,2048]{2,1,0:T(8,128)(2,1)} %bitcast.9), custom_call_target="tpu_custom_call" | custom-call | tf_op jit(solution)/shard_map/pallas_call | solution.py:180
  6.4 2.5 %collective-permute-done = f32[2,512,256]{2,1,0:T(8,128)S(1)} collective-permute-done((f32[2,512,256]{2,1,0:T(8,128)}, f32[2,512,256]{2,1,0:T(8,128)S(1)}, u32[]{:S(2)}, u32[]{:S(2)}) %collective-permute-start) | collective-permute-done | bytes 1048608 | tf_op jit(solution)/shard_map/ppermute | solution.py:409
  12.8 7.2 %all-to-all-start.1 = ((f32[8,64,512]{2,1,0:T(8,128)}), f32[8,64,512]{2,1,0:T(8,128)}, u32[]{:S(2)}, u32[]{:S(2)}) async-start(f32[8,64,512]{2,1,0:T(8,128)} %shard_map.84.refs_2_), calls=%async_computation.1 | async-start | bytes 2097152 | tf_op jit(solution)/shard_map/all_to_all | solution.py:425
  22.0 21.0 %collective-permute-done.1.refs_0_ = f32[8,1024]{1,0:T(8,128)S(1)} collective-permute-done((f32[8,1024]{1,0:T(8,128)S(1)}, f32[8,1024]{1,0:T(8,128)S(1)}, u32[]{:S(2)}, u32[]{:S(2)}) %collective-permute-start.1) | collective-permute-done | bytes 32800 | tf_op jit(solution)/shard_map/ppermute | solution.py:445
  44.0 7.5 %shard_map.86 = (f32[2,8,256]{2,1,0:T(8,128)S(1)}, f32[2,520,256]{2,1,0:T(8,128)}, f32[1,520,512]{2,1,0:T(8,128)}, f32[2,520,256]{2,1,0:T(8,128)}) custom-call(s32[4]{0:T(128)S(1)} %pad_add_fusion.owner_ref.refs_0_, bf16[520,1024]{1,0:T(8,128)(2,1)} %copy-done, bf16[3,1024,2048]{2,1,0:T(8,128)(2,1)} %bitcast.10), custom_call_target="tpu_custom_call" | custom-call | tf_op jit(solution)/shard_map/pallas_call | solution.py:180
  53.8 7.4 %shard_map.87 = (f32[2,8,256]{2,1,0:T(8,128)S(1)}, f32[2,520,256]{2,1,0:T(8,128)}, f32[1,520,512]{2,1,0:T(8,128)}, f32[2,520,256]{2,1,0:T(8,128)}) custom-call(s32[4]{0:T(128)S(1)} %pad_add_fusion.owner_ref.refs_0_, bf16[520,1024]{1,0:T(8,128)(2,1)} %copy-done, bf16[3,1024,2048]{2,1,0:T(8,128)(2,1)} %bitcast.11, f32[2,8,256]{2,1,0:T(8,128)S(1)} %get-tuple-element.31.refs_3_), custom_call_target="tpu_custom_call" | custom-call | tf_op jit(solution)/shard_map/pallas_call | solution.py:180
  65.1 13.4 %collective-permute-done.4.refs_2_ = f32[2,8,256]{2,1,0:T(8,128)S(1)} collective-permute-done((f32[2,8,256]{2,1,0:T(8,128)S(1)}, f32[2,8,256]{2,1,0:T(8,128)S(1)}, u32[]{:S(2)}, u32[]{:S(2)}) %collective-permute-start.4) | collective-permute-done | bytes 16416 | tf_op jit(solution)/shard_map/ppermute | solution.py:409
  79.8 5.5 %shard_map.89 = (f32[2,520,256]{2,1,0:T(8,128)}, f32[1,520,512]{2,1,0:T(8,128)}) custom-call(s32[4]{0:T(128)S(1)} %pad_add_fusion.owner_ref.refs_0_, bf16[520,1024]{1,0:T(8,128)(2,1)} %copy-done, bf16[3,1024,2048]{2,1,0:T(8,128)(2,1)} %bitcast.12, f32[8,32,512]{2,1,0:T(8,128)} %shard_map.88.refs_3_), custom_call_target="tpu_custom_call" | custom-call | tf_op jit(solution)/shard_map/pallas_call | solution.py:180
  85.4 6.5 %all-to-all-start = ((f32[8,32,512]{2,1,0:T(8,128)}), f32[8,32,512]{2,1,0:T(8,128)}, u32[]{:S(2)}, u32[]{:S(2)}) async-start(f32[8,32,512]{2,1,0:T(8,128)} %shard_map.88.refs_3_), calls=%async_computation | async-start | bytes 1048576 | tf_op jit(solution)/shard_map/all_to_all | solution.py:425
  91.9 5.5 %shard_map.90 = (f32[2,520,256]{2,1,0:T(8,128)}, f32[1,520,512]{2,1,0:T(8,128)}) custom-call(s32[4]{0:T(128)S(1)} %pad_add_fusion.owner_ref.refs_0_, bf16[520,1024]{1,0:T(8,128)(2,1)} %copy-done, bf16[3,1024,2048]{2,1,0:T(8,128)(2,1)} %bitcast.13, f32[2,520,256]{2,1,0:T(8,128)} %get-tuple-element.39.refs_3_), custom_call_target="tpu_custom_call" | custom-call | tf_op jit(solution)/shard_map/pallas_call | solution.py:180
  102.5 5.1 %all-to-all-done.refs_0_ = f32[8,32,512]{2,1,0:T(8,128)} async-done(((f32[8,32,512]{2,1,0:T(8,128)}), f32[8,32,512]{2,1,0:T(8,128)}, u32[]{:S(2)}, u32[]{:S(2)}) %all-to-all-start) | async-done | bytes 524320 | tf_op jit(solution)/shard_map/all_to_all | solution.py:425
  110.3 3.1 %shard_map.92 = (f32[32,512]{1,0:T(8,128)S(1)}, f32[32,512]{1,0:T(8,128)S(1)}, f32[32,512]{1,0:T(8,128)S(1)}, f32[32,512]{1,0:T(8,128)S(1)}, f32[32,512]{1,0:T(8...) custom-call(s32[1]{0:T(128)} %bitcast.me_ref, f32[8,32,512]{2,1,0:T(8,128)} %all-to-all-done.refs_0_, ...), custom_call_target="tpu_custom_call" | custom-call | tf_op jit(solution)/shard_map/pallas_call | solution.py:180
  116.1 2.8 %shard_map.93 = f32[8,32,512]{2,1,0:T(8,128)} custom-call(f32[2,520,256]{2,1,0:T(8,128)S(1)} %copy-done.3, f32[2,520,256]{2,1,0:T(8,128)} %collective-permute-done.15.refs_1_, f32[2,520,256]{2,1,0:T(8,128)} %collective-permute-done.16.refs_2_, f32[3,3,512]{2,1,0:T(4,128)S(1)} %copy-done.14, f32[32,512]{1,0:T(8,128)S(1)} %get-tuple-element.42.refs_4_.refs_0_), custom_call_target="tpu_custom_call" | custom-call | tf_op jit(solution)/shard_map/pallas_call | solution.py:180
  118.8 3.6 %all-to-all-start.2 = ((f32[8,32,512]{2,1,0:T(8,128)}), f32[8,32,512]{2,1,0:T(8,128)S(1)}, u32[]{:S(2)}, u32[]{:S(2)}) async-start(f32[8,32,512]{2,1,0:T(8,128)} %shard_map.93), calls=%async_computation.2 | async-start | bytes 1048576 | tf_op jit(solution)/shard_map/all_to_all | solution.py:425
  124.1 13.0 %all-to-all-done.2.in_ref = f32[8,32,512]{2,1,0:T(8,128)S(1)} async-done(((f32[8,32,512]{2,1,0:T(8,128)}), f32[8,32,512]{2,1,0:T(8,128)S(1)}, u32[]{:S(2)}, u32[]{:S(2)}) %all-to-all-start.2) | async-done | bytes 524320 | tf_op jit(solution)/shard_map/all_to_all | solution.py:425
  138.8 2.2 %shard_map.94 = f32[8,32,512]{2,1,0:T(8,128)} custom-call(f32[8,32,512]{2,1,0:T(8,128)S(1)} %all-to-all-done.2.in_ref, f32[17,32,256]{2,1,0:T(8,128)S(1)} %copy-done.11, bf16[2,256,256]{2,1,0:T(8,128)(2,1)S(1)} %copy-done.4, bf16[2,256,256]{2,1,0:T(8,128)(2,1)S(1)} %copy-done.9, f32[2,17,1,128]{3,2,1,0:T(1,128)S(1)} %copy-done.17), custom_call_target="tpu_custom_call" | custom-call | tf_op jit(solution)/shard_map/pallas_call | solution.py:180
  141.1 3.6 %all-to-all-start.3 = ((f32[8,32,512]{2,1,0:T(8,128)}), f32[8,32,512]{2,1,0:T(8,128)S(1)}, u32[]{:S(2)}, u32[]{:S(2)}) async-start(f32[8,32,512]{2,1,0:T(8,128)} %shard_map.94), calls=%async_computation.3 | async-start | bytes 1048576 | tf_op jit(solution)/shard_map/all_to_all | solution.py:425
  148.2 3.6 %collective-permute-done.8.refs_1_ = f32[32,512]{1,0:T(8,128)S(1)} collective-permute-done((f32[32,512]{1,0:T(8,128)}, f32[32,512]{1,0:T(8,128)S(1)}, u32[]{:S(2)}, u32[]{:S(2)}) %collective-permute-start.8) | collective-permute-done | bytes 65568 | tf_op jit(solution)/shard_map/ppermute | solution.py:409
  151.8 2.4 %collective-permute-start.11 = (f32[32,512]{1,0:T(8,128)S(1)}, f32[32,512]{1,0:T(8,128)S(1)}, u32[]{:S(2)}, u32[]{:S(2)}) collective-permute-start(f32[32,512]{1,0:T(8,128)S(1)} %copy-done.22), channel_id=1, source_target_pairs={{0,16},{4,20},{8,24},{12,28},{16,0},{20,4},{24,8},{28,12},{1,17},{... | collective-permute-start | bytes 196616 | tf_op jit(solution)/shard_map/ppermute | solution.py:409
  156.0 5.6 %collective-permute-start.12 = (f32[32,512]{1,0:T(8,128)}, f32[32,512]{1,0:T(8,128)S(1)}, u32[]{:S(2)}, u32[]{:S(2)}) collective-permute-start(f32[32,512]{1,0:T(8,128)} %get-tuple-element.47), channel_id=1, source_target_pairs={{0,20},{4,16},{8,28},{12,24},{16,4},{20,0},{24,12},{28,8},{1,21},{... | collective-permute-start | bytes 196616 | tf_op jit(solution)/shard_map/ppermute | solution.py:409
  162.2 3.3 %collective-permute-done.11.refs_4_ = f32[32,512]{1,0:T(8,128)S(1)} collective-permute-done((f32[32,512]{1,0:T(8,128)S(1)}, f32[32,512]{1,0:T(8,128)S(1)}, u32[]{:S(2)}, u32[]{:S(2)}) %collective-permute-start.11) | collective-permute-done | bytes 65568 | tf_op jit(solution)/shard_map/ppermute | solution.py:409
  166.0 3.0 %collective-permute-done.12.refs_5_ = f32[32,512]{1,0:T(8,128)S(1)} collective-permute-done((f32[32,512]{1,0:T(8,128)}, f32[32,512]{1,0:T(8,128)S(1)}, u32[]{:S(2)}, u32[]{:S(2)}) %collective-permute-start.12) | collective-permute-done | bytes 65568 | tf_op jit(solution)/shard_map/ppermute | solution.py:409
  169.0 3.5 %collective-permute-done.14.refs_7_ = f32[32,512]{1,0:T(8,128)S(1)} collective-permute-done((f32[32,512]{1,0:T(8,128)S(1)}, f32[32,512]{1,0:T(8,128)S(1)}, u32[]{:S(2)}, u32[]{:S(2)}) %collective-permute-start.14) | collective-permute-done | bytes 65568 | tf_op jit(solution)/shard_map/ppermute | solution.py:409
  172.5 3.0 %shard_map.95 = f32[512,512]{1,0:T(8,128)} custom-call(s32[1]{0:T(128)} %bitcast.me_ref, f32[32,512]{1,0:T(8,128)S(1)} %get-tuple-element.42.refs_4_.refs_0_, f32[32,512]{1,0:T(8,128)S(1)} %collective-permute-done.8.refs_1_, f32[32,512]{1,0:T(8,128)S(1)} %collective-permute-done.9.refs_2_, f32[32,512]{1,0:T(8,128)S(1)} %collective-permute-done.10.refs_3_, ...), custom_call_target="tpu_custom_call" | custom-call | tf_op jit(solution)/shard_map/pallas_call | solution.py:180
  (98 shorter events, 35.3 us)
Async XLA Ops:
  5.8 3.1 %collective-permute-start = (f32[2,512,256]{2,1,0:T(8,128)}, f32[2,512,256]{2,1,0:T(8,128)S(1)}, u32[]{:S(2)}, u32[]{:S(2)}) collective-permute-start(f32[2,512,256]{2,1,0:T(8,128)} %get-tuple-element.30), channel_id=1, source_target_pairs={{0,1},{1,0},{2,3},{3,2},{4,5},{5,4},{6,7},{7,6},{8,9},{9,8},{10,11... | collective-permute-start | bytes 3145736 | tf_op jit(solution)/shard_map/ppermute | solution.py:409
  12.8 72.7 %all-to-all-start.1 = ((f32[8,64,512]{2,1,0:T(8,128)}), f32[8,64,512]{2,1,0:T(8,128)}, u32[]{:S(2)}, u32[]{:S(2)}) async-start(f32[8,64,512]{2,1,0:T(8,128)} %shard_map.84.refs_2_), calls=%async_computation.1 | async-start | bytes 2097152 | tf_op jit(solution)/shard_map/all_to_all | solution.py:425
  19.9 23.1 %collective-permute-start.1 = (f32[8,1024]{1,0:T(8,128)S(1)}, f32[8,1024]{1,0:T(8,128)S(1)}, u32[]{:S(2)}, u32[]{:S(2)}) collective-permute-start(f32[8,1024]{1,0:T(8,128)S(1)} %shard_map.83.refs_3_), channel_id=1, source_target_pairs={{0,4},{4,8},{8,12},{12,16},{16,20},{20,24},{24,28},{28,0},{1,5},{5... | collective-permute-start | bytes 98312 | tf_op jit(solution)/shard_map/ppermute | solution.py:445
  51.5 10.3 %collective-permute-start.6 = (f32[2,520,256]{2,1,0:T(8,128)}, f32[2,520,256]{2,1,0:T(8,128)S(1)}, u32[]{:S(2)}, u32[]{:S(2)}) collective-permute-start(f32[2,520,256]{2,1,0:T(8,128)} %get-tuple-element.36), channel_id=1, source_target_pairs={{0,1},{1,0},{2,3},{3,2},{4,5},{5,4},{6,7},{7,6},{8,9},{9,8},{10,11... | collective-permute-start | bytes 3194888 | tf_op jit(solution)/shard_map/ppermute | solution.py:409
  51.6 13.3 %collective-permute-start.7 = (f32[1,520,512]{2,1,0:T(8,128)}, f32[1,520,512]{2,1,0:T(8,128)S(1)}, u32[]{:S(2)}, u32[]{:S(2)}) collective-permute-start(f32[1,520,512]{2,1,0:T(8,128)} %get-tuple-element.38), channel_id=1, source_target_pairs={{0,1},{1,0},{2,3},{3,2},{4,5},{5,4},{6,7},{7,6},{8,9},{9,8},{10,11... | collective-permute-start | bytes 3194888 | tf_op jit(solution)/shard_map/ppermute | solution.py:409
  52.1 26.5 %collective-permute-start.2 = (f32[2,520,256]{2,1,0:T(8,128)}, f32[2,520,256]{2,1,0:T(8,128)S(1)}, u32[]{:S(2)}, u32[]{:S(2)}) collective-permute-start(f32[2,520,256]{2,1,0:T(8,128)} %get-tuple-element.33), channel_id=1, source_target_pairs={{0,1},{1,0},{2,3},{3,2},{4,5},{5,4},{6,7},{7,6},{8,9},{9,8},{10,11... | collective-permute-start | bytes 3194888 | tf_op jit(solution)/shard_map/ppermute | solution.py:409
  52.2 26.4 %collective-permute-start.5 = (f32[2,512,256]{2,1,0:T(8,128)S(1)}, f32[2,512,256]{2,1,0:T(8,128)S(1)}, u32[]{:S(2)}, u32[]{:S(2)}) collective-permute-start(f32[2,512,256]{2,1,0:T(8,128)S(1)} %add.12.refs_1_), channel_id=1, source_target_pairs={{0,2},{1,3},{2,0},{3,1},{4,6},{5,7},{6,4},{7,5},{8,10},{9,11},{10,... | collective-permute-start | bytes 3145736 | tf_op jit(solution)/shard_map/ppermute | solution.py:409
  53.7 7.6 %collective-permute-start.3 = (f32[2,8,256]{2,1,0:T(8,128)S(1)}, f32[2,8,256]{2,1,0:T(8,128)S(1)}, u32[]{:S(2)}, u32[]{:S(2)}) collective-permute-start(f32[2,8,256]{2,1,0:T(8,128)S(1)} %get-tuple-element.31.refs_3_), channel_id=1, source_target_pairs={{0,1},{1,0},{2,3},{3,2},{4,5},{5,4},{6,7},{7,6},{8,9},{9,8},{10,11... | collective-permute-start | bytes 49160 | tf_op jit(solution)/shard_map/ppermute | solution.py:409
  61.3 17.3 %collective-permute-start.4 = (f32[2,8,256]{2,1,0:T(8,128)S(1)}, f32[2,8,256]{2,1,0:T(8,128)S(1)}, u32[]{:S(2)}, u32[]{:S(2)}) collective-permute-start(f32[2,8,256]{2,1,0:T(8,128)S(1)} %add.13.refs_5_), channel_id=1, source_target_pairs={{0,2},{1,3},{2,0},{3,1},{4,6},{5,7},{6,4},{7,5},{8,10},{9,11},{10,... | collective-permute-start | bytes 49160 | tf_op jit(solution)/shard_map/ppermute | solution.py:409
  63.3 52.1 %collective-permute-start.16 = (f32[2,520,256]{2,1,0:T(8,128)S(1)}, f32[2,520,256]{2,1,0:T(8,128)}, u32[]{:S(2)}, u32[]{:S(2)}) collective-permute-start(f32[2,520,256]{2,1,0:T(8,128)S(1)} %add.14.refs_6_), channel_id=1, source_target_pairs={{0,2},{1,3},{2,0},{3,1},{4,6},{5,7},{6,4},{7,5},{8,10},{9,11},{10,... | collective-permute-start | bytes 3194888 | tf_op jit(solution)/shard_map/ppermute | solution.py:409
  85.3 30.7 %collective-permute-start.15 = (f32[2,520,256]{2,1,0:T(8,128)}, f32[2,520,256]{2,1,0:T(8,128)}, u32[]{:S(2)}, u32[]{:S(2)}) collective-permute-start(f32[2,520,256]{2,1,0:T(8,128)} %get-tuple-element.39.refs_3_), channel_id=1, source_target_pairs={{0,1},{1,0},{2,3},{3,2},{4,5},{5,4},{6,7},{7,6},{8,9},{9,8},{10,11... | collective-permute-start | bytes 3194888 | tf_op jit(solution)/shard_map/ppermute | solution.py:409
  85.4 22.2 %all-to-all-start = ((f32[8,32,512]{2,1,0:T(8,128)}), f32[8,32,512]{2,1,0:T(8,128)}, u32[]{:S(2)}, u32[]{:S(2)}) async-start(f32[8,32,512]{2,1,0:T(8,128)} %shard_map.88.refs_3_), calls=%async_computation | async-start | bytes 1048576 | tf_op jit(solution)/shard_map/all_to_all | solution.py:425
  118.8 18.2 %all-to-all-start.2 = ((f32[8,32,512]{2,1,0:T(8,128)}), f32[8,32,512]{2,1,0:T(8,128)S(1)}, u32[]{:S(2)}, u32[]{:S(2)}) async-start(f32[8,32,512]{2,1,0:T(8,128)} %shard_map.93), calls=%async_computation.2 | async-start | bytes 1048576 | tf_op jit(solution)/shard_map/all_to_all | solution.py:425
  122.5 50.0 %collective-permute-start.18 = (f32[1,520,512]{2,1,0:T(8,128)S(1)}, f32[1,520,512]{2,1,0:T(8,128)}, u32[]{:S(2)}, u32[]{:S(2)}) collective-permute-start(f32[1,520,512]{2,1,0:T(8,128)S(1)} %add.15.refs_7_), channel_id=1, source_target_pairs={{0,2},{1,3},{2,0},{3,1},{4,6},{5,7},{6,4},{7,5},{8,10},{9,11},{10,... | collective-permute-start | bytes 3194888 | tf_op jit(solution)/shard_map/ppermute | solution.py:409
  124.0 48.4 %collective-permute-start.17 = (f32[1,520,512]{2,1,0:T(8,128)}, f32[1,520,512]{2,1,0:T(8,128)}, u32[]{:S(2)}, u32[]{:S(2)}) collective-permute-start(f32[1,520,512]{2,1,0:T(8,128)} %get-tuple-element.52), channel_id=1, source_target_pairs={{0,1},{1,0},{2,3},{3,2},{4,5},{5,4},{6,7},{7,6},{8,9},{9,8},{10,11... | collective-permute-start | bytes 3194888 | tf_op jit(solution)/shard_map/ppermute | solution.py:409
  138.8 33.6 %copy-start.5 = (f32[1,520,512]{2,1,0:T(8,128)S(1)}, f32[1,520,512]{2,1,0:T(8,128)}, u32[]{:S(2)}) copy-start(f32[1,520,512]{2,1,0:T(8,128)} %get-tuple-element.51.refs_9_) | copy-start | bytes 3194884
  141.1 31.4 %all-to-all-start.3 = ((f32[8,32,512]{2,1,0:T(8,128)}), f32[8,32,512]{2,1,0:T(8,128)S(1)}, u32[]{:S(2)}, u32[]{:S(2)}) async-start(f32[8,32,512]{2,1,0:T(8,128)} %shard_map.94), calls=%async_computation.3 | async-start | bytes 1048576 | tf_op jit(solution)/shard_map/all_to_all | solution.py:425
  144.7 7.1 %collective-permute-start.8 = (f32[32,512]{1,0:T(8,128)}, f32[32,512]{1,0:T(8,128)S(1)}, u32[]{:S(2)}, u32[]{:S(2)}) collective-permute-start(f32[32,512]{1,0:T(8,128)} %copy-done.26), channel_id=1, source_target_pairs={{0,4},{4,0},{8,12},{12,8},{16,20},{20,16},{24,28},{28,24},{1,5},{5... | collective-permute-start | bytes 196616 | tf_op jit(solution)/shard_map/ppermute | solution.py:409
  146.7 9.3 %collective-permute-start.9 = (f32[32,512]{1,0:T(8,128)}, f32[32,512]{1,0:T(8,128)S(1)}, u32[]{:S(2)}, u32[]{:S(2)}) collective-permute-start(f32[32,512]{1,0:T(8,128)} %copy-done.25), channel_id=1, source_target_pairs={{0,8},{4,12},{8,0},{12,4},{16,24},{20,28},{24,16},{28,20},{1,9},{5... | collective-permute-start | bytes 196616 | tf_op jit(solution)/shard_map/ppermute | solution.py:409
  148.2 13.4 %collective-permute-start.10 = (f32[32,512]{1,0:T(8,128)S(1)}, f32[32,512]{1,0:T(8,128)S(1)}, u32[]{:S(2)}, u32[]{:S(2)}) collective-permute-start(f32[32,512]{1,0:T(8,128)S(1)} %copy-done.24), channel_id=1, source_target_pairs={{0,12},{4,8},{8,4},{12,0},{16,28},{20,24},{24,20},{28,16},{1,13},{... | collective-permute-start | bytes 196616 | tf_op jit(solution)/shard_map/ppermute | solution.py:409
  151.8 13.7 %collective-permute-start.11 = (f32[32,512]{1,0:T(8,128)S(1)}, f32[32,512]{1,0:T(8,128)S(1)}, u32[]{:S(2)}, u32[]{:S(2)}) collective-permute-start(f32[32,512]{1,0:T(8,128)S(1)} %copy-done.22), channel_id=1, source_target_pairs={{0,16},{4,20},{8,24},{12,28},{16,0},{20,4},{24,8},{28,12},{1,17},{... | collective-permute-start | bytes 196616 | tf_op jit(solution)/shard_map/ppermute | solution.py:409
  156.0 12.9 %collective-permute-start.12 = (f32[32,512]{1,0:T(8,128)}, f32[32,512]{1,0:T(8,128)S(1)}, u32[]{:S(2)}, u32[]{:S(2)}) collective-permute-start(f32[32,512]{1,0:T(8,128)} %get-tuple-element.47), channel_id=1, source_target_pairs={{0,20},{4,16},{8,28},{12,24},{16,4},{20,0},{24,12},{28,8},{1,21},{... | collective-permute-start | bytes 196616 | tf_op jit(solution)/shard_map/ppermute | solution.py:409
  161.6 7.4 %collective-permute-start.13 = (f32[32,512]{1,0:T(8,128)}, f32[32,512]{1,0:T(8,128)S(1)}, u32[]{:S(2)}, u32[]{:S(2)}) collective-permute-start(f32[32,512]{1,0:T(8,128)} %get-tuple-element.48), channel_id=1, source_target_pairs={{0,24},{4,28},{8,16},{12,20},{16,8},{20,12},{24,0},{28,4},{1,25},{... | collective-permute-start | bytes 196616 | tf_op jit(solution)/shard_map/ppermute | solution.py:409
  165.5 7.0 %collective-permute-start.14 = (f32[32,512]{1,0:T(8,128)S(1)}, f32[32,512]{1,0:T(8,128)S(1)}, u32[]{:S(2)}, u32[]{:S(2)}) collective-permute-start(f32[32,512]{1,0:T(8,128)S(1)} %copy-done.20), channel_id=1, source_target_pairs={{0,28},{4,24},{8,20},{12,16},{16,12},{20,8},{24,4},{28,0},{1,29},{... | collective-permute-start | bytes 196616 | tf_op jit(solution)/shard_map/ppermute | solution.py:409
  (27 other events, 142.3 us)
where the time goes:
time: 177 us; the launch traced here: 176 us
  waiting for transfers between devices  70.3 us (40%)
  Pallas kernels  47.6 us (27%)
  starting transfers between devices  42.1 us (24%)
  local copies, waits for them, and re-layouts  12.1 us (7%)
  other arithmetic  3.11 us (2%)
    pallas_call x14, Pallas kernels, call(): pl.pallas_call(wrapped, out_shape=out_shape, in_specs=specs, out_specs=ja...  47.6 us
    ppermute x18, waiting for transfers between devices, exchanged(): return lax.ppermute(block, axis, [(i, i ^ stride) for i in range(size)])  31.2 us
    ppermute x1, waiting for transfers between devices, on_device(): lax.ppermute(rim, 'ctx', [(i, (i + 1) % owners) for i in range(owners)])  21 us
    all_to_all x4, starting transfers between devices, turn_over(): return lax.all_to_all(block, 'ctx', 0, 0, tiled=True)  20.9 us
    ppermute x18, starting transfers between devices, exchanged(): return lax.ppermute(block, axis, [(i, i ^ stride) for i in range(size)])  19.2 us
    all_to_all x4, waiting for transfers between devices, turn_over(): return lax.all_to_all(block, 'ctx', 0, 0, tiled=True)  18.1 us
    unnamed x56, local copies, waits for them, and re-layouts  12.1 us
  transfers between devices with their start and end apart: 23, of which 10 were waited for; matrix products, arithmetic and copies ran while one was open for 1% of the time, Pallas kernels for 20%

commit v1 on v0

--- a/solution.py
+++ b/solution.py
@@ -13,8 +13,7 @@
 LANES = 128
 SUBLANES = 8
 
-KERNEL_VMEM = 12 * 2**20
-PROJECT_VMEM = 53 * 2**20
+KERNEL_VMEM = 16 * 2**20
 VMEM_SPEC = pl.BlockSpec(memory_space=pltpu.VMEM)
 
 
@@ -108,7 +107,7 @@
 
 
 def forward_rows(in_ref, stage_ref, turns_ref):
-    channels = in_ref.shape[1]
+    channels = stage_ref.shape[1]
 
     def group(g, carry):
         rows = pl.ds(pl.multiple_of(g * SUBLANES, SUBLANES), SUBLANES)
@@ -125,22 +124,32 @@
     lax.fori_loop(0, channels // SUBLANES, group, 0)
 
 
-def convolve_kernel(
-    in_ref, spectrum_ref, forward_ref, inverse_ref, turns_ref, out_ref, stage_ref
-):
+def convolve_kernel(count, *refs):
+    scalars, refs = (refs[:1], refs[1:]) if count > 1 else ((), refs)
+    in_ref, turns_ref, *sources = refs[:5]
+    outs, (whole_ref, stage_ref, *held, sems) = refs[5 : 5 + count], refs[5 + count :]
+    copies = [
+        pltpu.make_async_copy(source, target, sems.at[i])
+        for i, (source, target) in enumerate(zip(sources, held))
+    ]
+    for copy in copies:
+        copy.start()
+    forward_ref, spectrum_ref, inverse_ref = held
     terms, channels, width = stage_ref.shape
     forward_rows(in_ref, stage_ref, turns_ref)
     rows = stage_ref[...].reshape(terms * channels, width)
+    copies[0].wait()
     signal = split_dot(rows, forward_ref)
+    copies[1].wait()
     other = spectrum_ref[...].reshape(terms * channels, width)
     s_real, s_imag = signal[:, :LANES], signal[:, LANES:]
     f_real, f_imag = other[:, :LANES], other[:, LANES:]
     product = jnp.concatenate(
         [s_real * f_real - s_imag * f_imag, s_real * f_imag + s_imag * f_real], axis=1
     )
+    copies[2].wait()
     stage_ref[...] = split_dot(product, inverse_ref).reshape(terms, channels, width)
-    _, _, tokens = in_ref.shape
-    per_source = tokens // LANES
+    per_source = in_ref.shape[2] // LANES
 
     def group(g, carry):
         group_rows = pl.ds(pl.multiple_of(g * SUBLANES, SUBLANES), SUBLANES)
@@ -151,11 +160,16 @@
             c, s = turns_ref[0, k], turns_ref[1, k]
             pairs.append((real * c - imag * s, imag * c + real * s))
         for m, block in enumerate(real_inverse(pairs)):
-            i = m % per_source
-            out_ref[m // per_source, group_rows, i * LANES : (i + 1) * LANES] = block
+            lanes = slice(m % per_source * LANES, (m % per_source + 1) * LANES)
+            whole_ref[m // per_source, group_rows, lanes] = block
         return carry
 
     lax.fori_loop(0, channels // SUBLANES, group, 0)
+    if count == 1:
+        outs[0][...] = whole_ref[...]
+    else:
+        for k, out_ref in enumerate(outs):
+            out_ref[...] = whole_ref[scalars[0][0] ^ k]
 
 
 def stage_shape(shape):
@@ -163,7 +177,7 @@
     return (sources * tokens // LANES // 2 + 1, channels, 2 * LANES)
 
 
-def call(kernel, out_shape, operands, scratch=(), after=(), scalar=None, hbm=(), vmem=KERNEL_VMEM):
+def call(kernel, out_shape, operands, scratch=(), after=(), scalar=None, hbm=()):
     wrapped = kernel
     n_scalar, n_in = int(scalar is not None), len(operands) + len(hbm)
     if after:
@@ -173,6 +187,7 @@
 
     anywhere = pl.BlockSpec(memory_space=pl.ANY)
     stays = pl.BlockSpec(memory_space=pltpu.HBM)
+    hbm = [pltpu.with_memory_space_constraint(array, pltpu.HBM) for array in hbm]
     specs = [VMEM_SPEC] * len(operands) + [stays] * len(hbm) + [anywhere] * len(after)
     lead = ()
     if scalar is not None:
@@ -183,7 +198,7 @@
         in_specs=specs,
         out_specs=jax.tree.map(lambda _: VMEM_SPEC, out_shape),
         scratch_shapes=list(scratch),
-        compiler_params=pltpu.CompilerParams(vmem_limit_bytes=vmem),
+        compiler_params=pltpu.CompilerParams(vmem_limit_bytes=KERNEL_VMEM),
     )(*lead, *operands, *hbm, *after)
 
 
@@ -191,49 +206,42 @@
     return jax.ShapeDtypeStruct(shape, jnp.float32)
 
 
-def spectrum_kernel(scale, offsets, in_ref, table_ref, turns_ref, *refs):
-    out_refs, stage_ref = refs[:-1], refs[-1]
-    terms, _, width = stage_ref.shape
-    forward_rows(in_ref, stage_ref, turns_ref)
-    for out_ref, first in zip(out_refs, offsets):
-        count = out_ref.shape[1]
-        rows = stage_ref[:, first : first + count, :].reshape(terms * count, width)
-        out_ref[...] = (split_dot(rows, table_ref) * scale).reshape(terms, count, width)
-
-
-def spectrum(received, forward, turns, chunks, after):
-    owners, channels, tokens = received.shape
-    terms, _, width = stage_shape(received.shape)
+def spectrum_kernel(scale, first, in_ref, table_ref, turns_ref, out_ref):
+    terms, channels, width = out_ref.shape
+    forward_rows(in_ref.at[:, first : first + channels, :], out_ref, turns_ref)
+    rows = out_ref[...].reshape(terms * channels, width)
+    out_ref[...] = (split_dot(rows, table_ref) * scale).reshape(terms, channels, width)
+
+
+def spectrum(received, first, channels, forward, turns, after):
+    owners, _, tokens = received.shape
     return call(
-        functools.partial(
-            spectrum_kernel, 1.0 / (owners * tokens), [start // owners for start, _ in chunks]
+        functools.partial(spectrum_kernel, 1.0 / (owners * tokens), first),
+        f32(*stage_shape((owners, channels, tokens))),
+        (received, forward, turns),
+        after=after,
+    )
+
+
+def convolve(received, taps, forward, inverse, turns, me=None, after=()):
+    vmem = lambda array: pltpu.VMEM(array.shape, array.dtype)
+    count = 1 if me is None else received.shape[0]
+    shapes = [f32(*received.shape)] if me is None else [f32(*received.shape[1:])] * count
+    return call(
+        functools.partial(convolve_kernel, count),
+        shapes,
+        (received, turns),
+        (
+            vmem(received),
+            pltpu.VMEM(stage_shape(received.shape), jnp.float32),
+            vmem(forward),
+            vmem(taps),
+            vmem(inverse),
+            pltpu.SemaphoreType.DMA((3,)),
         ),
-        [f32(terms, size // owners, width) for _, size in chunks],
-        (received, forward, turns),
-        scratch=[pltpu.VMEM((terms, channels, width), jnp.float32)],
-        after=after,
-    )
-
-
-def convolve_apart_kernel(me_ref, *refs):
-    ins, outs, (stage_ref, whole_ref) = refs[:5], refs[5:-2], refs[-2:]
-    convolve_kernel(*ins, whole_ref, stage_ref)
-    for k, out_ref in enumerate(outs):
-        out_ref[...] = whole_ref[me_ref[0] ^ k]
-
-
-def convolve(received, filter_spectrum, forward, inverse, turns, me=None, after=()):
-    operands = (received, filter_spectrum, forward, inverse, turns)
-    stage = pltpu.VMEM(stage_shape(received.shape), jnp.float32)
-    if me is None:
-        return call(convolve_kernel, f32(*received.shape), operands, (stage,), after)
-    return call(
-        convolve_apart_kernel,
-        [f32(*received.shape[1:])] * received.shape[0],
-        operands,
-        (stage, pltpu.VMEM(received.shape, jnp.float32)),
         after,
         me,
+        (forward, taps, inverse),
     )
 
 
@@ -289,7 +297,6 @@
         after=after,
         scalar=owners,
         hbm=(rows, weight) if load_rows else (weight,),
-        vmem=PROJECT_VMEM,
     )
 
 
@@ -324,12 +331,12 @@
 
 
 def gate_kernel(offset, *refs):
-    parts, (tap_ref, out_ref, ext_ref) = refs[:-3], refs[-3:]
+    parts, (taps_ref, out_ref, ext_ref) = refs[:-3], refs[-3:]
     width = parts[0].shape[2]
     _, channels, tokens = out_ref.shape
     for at in range(0, width, LANES):
         cols = slice(at, at + LANES)
-        taps = tap_ref.at[:, :, offset + at : offset + at + LANES]
+        taps = taps_ref.at[:, :, offset + at : offset + at + LANES]
         for slot in range(2):
             fill_extended(ext_ref, slot, cols, parts)
         for start in range(0, tokens, LANES):
@@ -349,7 +356,7 @@
         f32(owners, width // owners, rows - SUBLANES),
         (*parts, taps),
         scratch=[pltpu.VMEM((2, rows, LANES), jnp.float32)],
-        after=after,
+        after=tuple(after),
     )
 
 
@@ -373,35 +380,41 @@
                 ] = block[piece * channels : (piece + 1) * channels]
 
 
-def end_kernel(chunks, apart, me_ref, *refs):
-    n = len(chunks)
-    owners = refs[0].shape[0] if not apart else apart
-    count = n - 1 + owners if apart else n
-    parts, (tap_ref, out_ref, ext_ref, whole_ref) = refs[count:-4], refs[-4:]
-    tokens, _ = out_ref.shape
-    blocks = list(refs[:n])
-    if apart:
-        for k in range(owners):
-            whole_ref[me_ref[0] ^ k] = refs[k][...]
-        blocks = [whole_ref] + list(refs[owners:count])
-    for ref, (start, width) in zip(blocks, chunks):
-        channels = ref.shape[1]
-        for at in range(start, start + width, LANES):
+def rows_of(ref, channel, row):
+    channels = ref.shape[1]
+    first, held = channel // channels, LANES // channels
+    return ref[first : first + held, :, row : row + LANES].reshape(LANES, LANES).T
+
+
+def query_kernel(width, owners, me_ref, *refs):
+    blocks, parts = refs[:owners], refs[owners:-4]
+    tap_ref, out_ref, ext_ref, whole_ref = refs[-4:]
+    for k in range(owners):
+        whole_ref[me_ref[0] ^ k] = blocks[k][...]
+    for at in range(0, out_ref.shape[1], LANES):
+        cols = slice(at, at + LANES)
+        fill_extended(ext_ref, 0, cols, parts)
+        taps = tap_ref.at[:, :, cols]
+        for row in range(0, out_ref.shape[0], LANES):
+            query = short_filtered(taps, 0, ext_ref, 0, row, LANES)
+            if at < width:
+                query = query * rows_of(whole_ref, at, row)
+            out_ref[row : row + LANES, cols] = query
+
+
+def end_kernel(first, query_ref, convolved_ref, out_ref):
+    tokens, width = out_ref.shape
+    out_ref[:, :first] = query_ref[:, :first]
+    for row in range(0, tokens, LANES):
+        rows = slice(row, row + LANES)
+        for at in range(first, width, LANES):
             cols = slice(at, at + LANES)
-            fill_extended(ext_ref, 0, cols, parts)
-            taps = tap_ref.at[:, :, cols]
-            held = LANES // channels
-            first = (at - start) // channels
-            for row in range(0, tokens, LANES):
-                query = short_filtered(taps, 0, ext_ref, 0, row, LANES)
-                block = ref[first : first + held, :, row : row + LANES].reshape(LANES, LANES)
-                out_ref[row : row + LANES, cols] = query * block.T
-
-
-def chunk_list(width, owners):
-    grain = max(LANES, SUBLANES * owners)
-    size = max(grain, width // 2)
-    return tuple((start, size) for start in range(0, width, size))
+            out_ref[rows, cols] = query_ref[rows, cols] * rows_of(convolved_ref, at - first, row)
+
+
+def halves(width, owners):
+    size = max(width // 2, max(LANES, SUBLANES * owners))
+    return ((0, size), (size, width - size))
 
 
 def exchanged(block, axis, stride):
@@ -413,7 +426,7 @@
     tokens, depth = sequence.shape
     width = long_filter.shape[1]
     owners = lax.axis_size("ctx")
-    chunks = chunk_list(width, owners)
+    chunks = halves(width, owners)
     weight = w_proj.transpose(1, 0, 2)
     col = lax.axis_index("col")
     owner = jnp.stack([col ^ d for d in range(4)]).astype(jnp.int32)
@@ -436,82 +449,84 @@
         [(3, tokens, both, start, size), (2, tokens, both, start, size)],
         load_rows=True,
     )
-    first_far = kept + swap(sent, 1)
-    first_body = swap(first_far, 2)
-
-    rim = call(
-        last_rows_kernel, f32(SUBLANES, depth), (sequence[tokens - SUBLANES :],), after=(first_far,)
-    )
-    rim_got = lax.ppermute(rim, "ctx", [(i, (i + 1) % owners) for i in range(owners)])
+    sent_far = swap(sent, 1)
+
     packed = call(
         functools.partial(pack_kernel, chunks),
         f32(owners, width // owners, tokens),
         (long_filter, skip_gain[None]),
-        after=(rim,),
+        after=(sent,),
         scalar=(lax.axis_index("ctx") == 0)[None].astype(jnp.int32),
     )
+    rim = call(
+        last_rows_kernel, f32(SUBLANES, depth), (sequence[tokens - SUBLANES :],), after=(sent,)
+    )
+    rim_got = lax.ppermute(rim, "ctx", [(i, (i + 1) % owners) for i in range(owners)])
+    first_far = kept + sent_far
+    first_body = swap(first_far, 2)
     filter_got = turn_over(packed)
     extended = call(
         extend_kernel,
         jax.ShapeDtypeStruct((rows, depth), sequence.dtype),
         (rim_got, sequence),
-        after=(packed,),
-    )
-
-    def pieces(far, near):
-        listed = [(far, SUBLANES, both, start, size)]
-        listed += [(far, rows, both, start, size) for start, size in chunks[1:]]
-        return listed + [(far, rows, (0,), 0, width), (near, rows, both, start, size)]
-
-    sent = project(extended, weight, owner, width, pieces(3, 1))
-    kept = project(extended, weight, owner, width, pieces(2, 0), after=sent[:1])
-    got = [swap(s, 1) for s in sent]
-    far_sums = [k + g for k, g in zip(kept[:-1], got)]
-    far = [swap(s, 2) for s in far_sums]
-    far_parts = [(far[0], first_body)] + [(f,) for f in far[1:]]
-    parts = [(kept[-1], got[-1])]
-
-    def gated_chunk(index, after):
-        part = (*parts[index], *far_parts[index])
-        return gate(part, short_filter, chunks[index][0], owners, after)
-
-    gated = gated_chunk(0, tuple(far_sums))
-
-    def pieces(near):
-        listed = [(near, rows, both, start, size) for start, size in chunks[1:]]
-        return listed + [(near, rows, (0,), 0, width)]
-
-    sent = project(extended, weight, owner, width, pieces(1), after=(gated,))
-    kept = project(extended, weight, owner, width, pieces(0), after=sent[:1])
-    parts += [(k, swap(s, 1)) for k, s in zip(kept, sent)]
-    spectra = spectrum(filter_got, forward, turns, chunks, tuple(kept[:1]))
-    last = len(chunks) - 1
+        after=(packed, first_far),
+    )
+
+    def both_ways(pieces, after=()):
+        listed = [(3 - 2 * y, *piece) for y, *piece in pieces]
+        listed += [(2 - 2 * y, *piece) for y, *piece in pieces]
+        results = project(extended, weight, owner, width, listed, after)
+        sent, kept = results[: len(pieces)], results[len(pieces) :]
+        return [(k, swap(s, 1)) for k, s in zip(kept, sent)]
+
+    first, second = chunks
+    query = (rows, (0,), 0, width)
+    far_rim, far_second = both_ways([(0, SUBLANES, both, *first), (0, rows, both, *second)])
+    near_first, far_query = both_ways([(1, rows, both, *first), (0, *query)], (far_second[0],))
+    got_rim = swap(far_rim[0] + far_rim[1], 2)
+    sum_second = far_second[0] + far_second[1]
+    got_second = swap(sum_second, 2)
+    sum_query = far_query[0] + far_query[1]
+    got_query = swap(sum_query, 2)
+
+    channels = [size // owners for _, size in chunks]
+    gated = gate(
+        (*near_first, got_rim, first_body),
+        short_filter,
+        first[0],
+        owners,
+        after=(sum_second, sum_query),
+    )
+    arrived = turn_over(gated)
+    near_second = both_ways([(1, rows, both, *second)], (gated,))[0]
+    taps = [near_second[0]]
+    for index in range(2):
+        begin = index * channels[0]
+        taps.append(
+            spectrum(filter_got, begin, channels[index], forward, turns, (taps[-1],))
+        )
+    gated = gate((*near_second, got_second), short_filter, second[0], owners, after=taps[2:])
     me = lax.axis_index("ctx")[None].astype(jnp.int32)
-    convolved, done = [], spectra[0]
-    for index in range(len(chunks)):
-        arrived = turn_over(gated)
-        apart = index == 0 < last
-        done = convolve(
-            arrived, spectra[index], forward, inverse, turns, me if apart else None
-        )
-        if index < last:
-            gated = gated_chunk(index + 1, tuple(done[:1]) if apart else (done,))
-        if apart:
-            convolved.append(done[0])
-            for k in range(1, owners):
-                convolved.append(exchanged(done[k], "ctx", k))
-        else:
-            convolved.append(turn_over(done))
-    return call(
-        functools.partial(end_kernel, chunks, owners if last else 0),
+    apart = convolve(arrived, taps[1], forward, inverse, turns, me, (gated,))
+    arrived = turn_over(gated)
+    back = [apart[0]]
+    for k in range(1, owners):
+        back.append(exchanged(apart[k], "ctx", k))
+    done = convolve(arrived, taps[2], forward, inverse, turns)[0]
+    convolved = turn_over(done)
+    near_query = both_ways([(1, *query)], (done,))[0]
+    queries = call(
+        functools.partial(query_kernel, first[1], owners),
         f32(tokens, width),
-        (*convolved, *parts[-1], *far_parts[-1], short_filter),
+        (*back, *near_query, got_query, short_filter),
         scratch=[
             pltpu.VMEM((1, rows, LANES), jnp.float32),
-            pltpu.VMEM((owners, chunks[0][1] // owners, tokens), jnp.float32),
+            pltpu.VMEM((owners, channels[0], tokens), jnp.float32),
         ],
         scalar=me,
-    )
+        after=(done,),
+    )
+    return call(functools.partial(end_kernel, first[1]), f32(tokens, width), (queries, convolved))
 
 
 def solution(mesh):

time: 177 us -> 152 us (0.86)
  waiting for transfers between devices: 70.3 us -> 37.9 us
  blocking collectives: 0 us -> 18.5 us
  starting transfers between devices: 42.1 us -> 34.1 us
  Pallas kernels: 47.6 us -> 42.2 us
  other arithmetic: 3.11 us -> 6.29 us
    ppermute x1, waiting for transfers between devices: 21 us -> 1.43 us  [on_device(): lax.ppermute(rim, 'ctx', [(i, (i + 1) % owners) for i in range(owners)])]
    all_to_all x0 -> x1, blocking collectives: none -> 18.5 us  [turn_over(): return lax.all_to_all(block, 'ctx', 0, 0, tiled=True)]
    all_to_all x4 -> x3, waiting for transfers between devices: 18.1 us -> 3.15 us  [turn_over(): return lax.all_to_all(block, 'ctx', 0, 0, tiled=True)]
    all_to_all x4 -> x3, starting transfers between devices: 20.9 us -> 11.7 us  [turn_over(): return lax.all_to_all(block, 'ctx', 0, 0, tiled=True)]
    pallas_call x14 -> x16, Pallas kernels: 47.6 us -> 42.2 us  [call(): pl.pallas_call(wrapped, out_shape=out_shape, in_specs=specs, out_specs=ja...]
    add x4, other arithmetic: 3.04 us -> 6.21 us  [the longest x1 2.34 us: on_device(): sum_second = far_second[0] + far_second[1]]
    ppermute x18, waiting for transfers between devices: 31.2 us -> 33.3 us  [exchanged(): return lax.ppermute(block, axis, [(i, i ^ stride) for i in range(size)])]
    unnamed x56 -> x52, local copies, waits for them, and re-layouts: 12.1 us -> 11.5 us
  transfers between devices with their start and end apart: 23 -> 22, of which waited for: 10 -> 7; matrix products, arithmetic and copies ran while one was open for 1% -> 4% of each run, Pallas kernels for 20% -> 19%
where the time goes in v1:
time: 152 us; the launch traced here: 151 us
  Pallas kernels  42.2 us (28%)
  waiting for transfers between devices  37.9 us (25%)
  starting transfers between devices  34.1 us (22%)
  blocking collectives  18.5 us (12%)
  local copies, waits for them, and re-layouts  11.5 us (8%)
  other arithmetic  6.29 us (4%)
    pallas_call x16, Pallas kernels, call(): pl.pallas_call(wrapped, out_shape=out_shape, in_specs=specs, out_specs=ja...  42.2 us
    ppermute x18, waiting for transfers between devices, exchanged(): return lax.ppermute(block, axis, [(i, i ^ stride) for i in range(size)])  33.3 us
    ppermute x18, starting transfers between devices, exchanged(): return lax.ppermute(block, axis, [(i, i ^ stride) for i in range(size)])  19.9 us
    all_to_all x1, blocking collectives, turn_over(): return lax.all_to_all(block, 'ctx', 0, 0, tiled=True)  18.5 us
    all_to_all x3, starting transfers between devices, turn_over(): return lax.all_to_all(block, 'ctx', 0, 0, tiled=True)  11.7 us
    unnamed x52, local copies, waits for them, and re-layouts  11.5 us
    all_to_all x3, waiting for transfers between devices, turn_over(): return lax.all_to_all(block, 'ctx', 0, 0, tiled=True)  3.15 us
  transfers between devices with their start and end apart: 22, of which 7 were waited for; matrix products, arithmetic and copies ran while one was open for 4% of the time, Pallas kernels for 19%

profile of v1, /device:TPU:0, one launch (start us, length us, event | category | flops | bytes accessed | tf_op | source)
XLA Modules:
  0.0 150.7 jit_solution(6128908876433005333)
XLA Ops:
  0.1 4.7 %shard_map.82 = (f32[2,512,256]{2,1,0:T(8,128)S(1)}, f32[2,512,256]{2,1,0:T(8,128)S(1)}) custom-call(s32[4]{0:T(128)S(1)} %pad_add_fusion.owner_ref.refs_0_, bf16[512,1024]{1,0:T(8,128)(2,1)} %refs_1_.4, bf16[3,1024,2048]{2,1,0:T(8,128)(2,1)} %bitcast.9), custom_call_target="tpu_custom_call" | custom-call | tf_op jit(solution)/shard_map/pallas_call | solution.py:195
  6.3 2.5 %collective-permute-start = (f32[8,1024]{1,0:T(8,128)S(1)}, f32[8,1024]{1,0:T(8,128)S(1)}, u32[]{:S(2)}, u32[]{:S(2)}) collective-permute-start(f32[8,1024]{1,0:T(8,128)S(1)} %shard_map.83), channel_id=1, source_target_pairs={{0,4},{4,8},{8,12},{12,16},{16,20},{20,24},{24,28},{28,0},{1,5},{5... | collective-permute-start | bytes 98312 | tf_op jit(solution)/shard_map/ppermute | solution.py:464
  10.2 2.3 %add.12.refs_3_ = f32[2,512,256]{2,1,0:T(8,128)} add(f32[2,512,256]{2,1,0:T(8,128)S(1)} %copy-done.22, f32[2,512,256]{2,1,0:T(8,128)} %collective-permute-done.1) | non-fusion elementwise | flops 262144 | bytes 3145728 | tf_op jit(solution)/shard_map/add | solution.py:465
  14.0 5.8 %shard_map.86 = (f32[2,8,256]{2,1,0:T(8,128)S(1)}, f32[2,520,256]{2,1,0:T(8,128)}, f32[2,8,256]{2,1,0:T(8,128)S(1)}, f32[2,520,256]{2,1,0:T(8,128)S(1)}) custom-call(s32[4]{0:T(128)S(1)} %pad_add_fusion.owner_ref.refs_0_, bf16[520,1024]{1,0:T(8,128)(2,1)S(1)} %shard_map.85.refs_0_.refs_1_, bf16[3,1024,2048]{2,1,0:T(8,128)(2,1)} %bitcast.10), custom_call_target="tpu_custom_call" | custom-call | tf_op jit(solution)/shard_map/pallas_call | solution.py:195
  19.9 6.6 %shard_map.87 = (f32[2,520,256]{2,1,0:T(8,128)}, f32[1,520,512]{2,1,0:T(8,128)}, f32[2,520,256]{2,1,0:T(8,128)S(1)}, f32[1,520,512]{2,1,0:T(8,128)S(1)}) custom-call(s32[4]{0:T(128)S(1)} %pad_add_fusion.owner_ref.refs_0_, bf16[520,1024]{1,0:T(8,128)(2,1)S(1)} %shard_map.85.refs_0_.refs_1_, bf16[3,1024,2048]{2,1,0:T(8,128)(2,1)} %bitcast.11, ...), custom_call_target="tpu_custom_call" | custom-call | tf_op jit(solution)/shard_map/pallas_call | solution.py:195
  30.5 4.4 %all-to-all-start.1 = ((f32[8,64,512]{2,1,0:T(8,128)}), f32[8,64,512]{2,1,0:T(8,128)S(1)}, u32[]{:S(2)}, u32[]{:S(2)}) async-start(f32[8,64,512]{2,1,0:T(8,128)} %shard_map.84.refs_2_), calls=%async_computation.1 | async-start | bytes 2097152 | tf_op jit(solution)/shard_map/all_to_all | solution.py:438
  36.6 2.3 %add.14.refs_5_ = f32[2,520,256]{2,1,0:T(8,128)} add(f32[2,520,256]{2,1,0:T(8,128)S(1)} %get-tuple-element.29.refs_3_, f32[2,520,256]{2,1,0:T(8,128)} %collective-permute-done.6) | non-fusion elementwise | flops 266240 | bytes 3194880 | tf_op jit(solution)/shard_map/add | solution.py:487
  42.0 13.6 %collective-permute-done.4.refs_2_ = f32[2,8,256]{2,1,0:T(8,128)S(1)} collective-permute-done((f32[2,8,256]{2,1,0:T(8,128)S(1)}, f32[2,8,256]{2,1,0:T(8,128)S(1)}, u32[]{:S(2)}, u32[]{:S(2)}) %collective-permute-start.4) | collective-permute-done | bytes 16416 | tf_op jit(solution)/shard_map/ppermute | solution.py:422
  55.6 2.9 %shard_map.88.refs_3_ = f32[8,32,512]{2,1,0:T(8,128)} custom-call(f32[2,520,256]{2,1,0:T(8,128)S(1)} %copy-done.19, f32[2,520,256]{2,1,0:T(8,128)} %collective-permute-done.2.refs_1_, f32[2,8,256]{2,1,0:T(8,128)S(1)} %collective-permute-done.4.refs_2_, f32[2,512,256]{2,1,0:T(8,128)} %collective-permute-done.5.refs_3_, f32[3,3,512]{2,1,0:T(4,128)S(1)} %copy-done.24, ...), custom_call_target="tpu_custom_call" | custom-call | tf_op jit(solution)/shard_map/pallas_call | solution.py:195
  58.5 4.8 %shard_map.89 = (f32[2,520,256]{2,1,0:T(8,128)}, f32[2,520,256]{2,1,0:T(8,128)S(1)}) custom-call(s32[4]{0:T(128)S(1)} %pad_add_fusion.owner_ref.refs_0_, bf16[520,1024]{1,0:T(8,128)(2,1)S(1)} %shard_map.85.refs_0_.refs_1_, bf16[3,1024,2048]{2,1,0:T(8,128)(2,1)} %bitcast.12, f32[8,32,512]{2,1,0:T(8,128)} %shard_map.88.refs_3_), custom_call_target="tpu_custom_call" | custom-call | tf_op jit(solution)/shard_map/pallas_call | solution.py:195
  66.9 11.1 %collective-permute-done.9.refs_2_ = f32[2,520,256]{2,1,0:T(8,128)} collective-permute-done((f32[2,520,256]{2,1,0:T(8,128)}, f32[2,520,256]{2,1,0:T(8,128)}, u32[]{:S(2)}, u32[]{:S(2)}) %collective-permute-start.9) | collective-permute-done | bytes 1064992 | tf_op jit(solution)/shard_map/ppermute | solution.py:422
  80.1 18.5 %all_to_all.20.refs_0_ = f32[8,32,512]{2,1,0:T(8,128)} all-to-all(f32[8,32,512]{2,1,0:T(8,128)S(1)} %shard_map.92.refs_6_), channel_id=1, replica_groups=mesh['ctx'=8,'col'=4] {'ctx'}, dimensions={0} | all-to-all | bytes 1048576 | tf_op jit(solution)/shard_map/all_to_all | solution.py:438
  98.6 3.7 %all-to-all-start = ((f32[8,32,512]{2,1,0:T(8,128)}), f32[8,32,512]{2,1,0:T(8,128)S(1)}, u32[]{:S(2)}, u32[]{:S(2)}) async-start(f32[8,32,512]{2,1,0:T(8,128)} %shard_map.88.refs_3_), calls=%async_computation | async-start | bytes 1048576 | tf_op jit(solution)/shard_map/all_to_all | solution.py:438
  104.9 3.3 %shard_map.94.refs_3_.refs_13_ = f32[8,32,512]{2,1,0:T(8,128)} custom-call(f32[8,32,512]{2,1,0:T(8,128)S(1)} %copy-done.11, f32[2,17,1,128]{3,2,1,0:T(1,128)S(1)} %copy-done.23, bf16[2,256,256]{2,1,0:T(8,128)(2,1)} %constant.32.refs_1_.refs_3_.refs_2_, f32[17,32,256]{2,1,0:T(8,128)} %copy-done.1, bf16[2,256,256]{2,1,0:T(8,128)(2,1)} %constant.39.refs_5_.refs_4_), custom_call_target="tpu_custom_call" | custom-call | tf_op jit(solution)/shard_map/pallas_call | solution.py:195
  108.2 4.0 %shard_map.95 = (f32[1,520,512]{2,1,0:T(8,128)}, f32[1,520,512]{2,1,0:T(8,128)S(1)}) custom-call(s32[4]{0:T(128)S(1)} %pad_add_fusion.owner_ref.refs_0_, bf16[520,1024]{1,0:T(8,128)(2,1)S(1)} %shard_map.85.refs_0_.refs_1_, bf16[3,1024,2048]{2,1,0:T(8,128)(2,1)} %bitcast.13, f32[8,32,512]{2,1,0:T(8,128)} %shard_map.94.refs_3_.refs_13_), custom_call_target="tpu_custom_call" | custom-call | tf_op jit(solution)/shard_map/pallas_call | solution.py:195
  113.2 3.1 %all-to-all-done.refs_1_ = f32[8,32,512]{2,1,0:T(8,128)S(1)} async-done(((f32[8,32,512]{2,1,0:T(8,128)}), f32[8,32,512]{2,1,0:T(8,128)S(1)}, u32[]{:S(2)}, u32[]{:S(2)}) %all-to-all-start) | async-done | bytes 524320 | tf_op jit(solution)/shard_map/all_to_all | solution.py:438
  117.1 3.6 %all-to-all-start.3 = ((f32[8,32,512]{2,1,0:T(8,128)}), f32[8,32,512]{2,1,0:T(8,128)S(1)}, u32[]{:S(2)}, u32[]{:S(2)}) async-start(f32[8,32,512]{2,1,0:T(8,128)} %shard_map.94.refs_3_.refs_13_), calls=%async_computation.3 | async-start | bytes 1048576 | tf_op jit(solution)/shard_map/all_to_all | solution.py:438
  121.8 2.6 %shard_map.93 = (f32[32,512]{1,0:T(8,128)S(1)}, f32[32,512]{1,0:T(8,128)S(1)}, f32[32,512]{1,0:T(8,128)S(1)}, f32[32,512]{1,0:T(8,128)S(1)}, f32[32,512]{1,0:T(8...) custom-call(s32[1]{0:T(128)} %bitcast.refs_0_, f32[8,32,512]{2,1,0:T(8,128)S(1)} %copy-done.10, ...), custom_call_target="tpu_custom_call" | custom-call | tf_op jit(solution)/shard_map/pallas_call | solution.py:195
  124.4 2.1 %collective-permute-start.10 = (f32[32,512]{1,0:T(8,128)S(1)}, f32[32,512]{1,0:T(8,128)S(1)}, u32[]{:S(2)}, u32[]{:S(2)}) collective-permute-start(f32[32,512]{1,0:T(8,128)S(1)} %get-tuple-element.40), channel_id=1, source_target_pairs={{0,4},{4,0},{8,12},{12,8},{16,20},{20,16},{24,28},{28,24},{1,5},{5... | collective-permute-start | bytes 196616 | tf_op jit(solution)/shard_map/ppermute | solution.py:422
  128.1 2.8 %collective-permute-start.13 = (f32[32,512]{1,0:T(8,128)S(1)}, f32[32,512]{1,0:T(8,128)S(1)}, u32[]{:S(2)}, u32[]{:S(2)}) collective-permute-start(f32[32,512]{1,0:T(8,128)S(1)} %get-tuple-element.43), channel_id=1, source_target_pairs={{0,16},{4,20},{8,24},{12,28},{16,0},{20,4},{24,8},{28,12},{1,17},{... | collective-permute-start | bytes 196616 | tf_op jit(solution)/shard_map/ppermute | solution.py:422
  130.9 2.2 %collective-permute-start.14 = (f32[32,512]{1,0:T(8,128)S(1)}, f32[32,512]{1,0:T(8,128)S(1)}, u32[]{:S(2)}, u32[]{:S(2)}) collective-permute-start(f32[32,512]{1,0:T(8,128)S(1)} %get-tuple-element.44), channel_id=1, source_target_pairs={{0,20},{4,16},{8,28},{12,24},{16,4},{20,0},{24,12},{28,8},{1,21},{... | collective-permute-start | bytes 196616 | tf_op jit(solution)/shard_map/ppermute | solution.py:422
  133.1 2.6 %collective-permute-start.15 = (f32[32,512]{1,0:T(8,128)S(1)}, f32[32,512]{1,0:T(8,128)S(1)}, u32[]{:S(2)}, u32[]{:S(2)}) collective-permute-start(f32[32,512]{1,0:T(8,128)S(1)} %get-tuple-element.45), channel_id=1, source_target_pairs={{0,24},{4,28},{8,16},{12,20},{16,8},{20,12},{24,0},{28,4},{1,25},{... | collective-permute-start | bytes 196616 | tf_op jit(solution)/shard_map/ppermute | solution.py:422
  135.8 2.3 %collective-permute-start.16 = (f32[32,512]{1,0:T(8,128)S(1)}, f32[32,512]{1,0:T(8,128)S(1)}, u32[]{:S(2)}, u32[]{:S(2)}) collective-permute-start(f32[32,512]{1,0:T(8,128)S(1)} %get-tuple-element.46), channel_id=1, source_target_pairs={{0,28},{4,24},{8,20},{12,16},{16,12},{20,8},{24,4},{28,0},{1,29},{... | collective-permute-start | bytes 196616 | tf_op jit(solution)/shard_map/ppermute | solution.py:422
  138.1 5.6 %collective-permute-done.13.refs_5_ = f32[32,512]{1,0:T(8,128)S(1)} collective-permute-done((f32[32,512]{1,0:T(8,128)S(1)}, f32[32,512]{1,0:T(8,128)S(1)}, u32[]{:S(2)}, u32[]{:S(2)}) %collective-permute-start.13) | collective-permute-done | bytes 65568 | tf_op jit(solution)/shard_map/ppermute | solution.py:422
  (95 shorter events, 32.9 us)
Async XLA Ops:
  5.8 4.4 %collective-permute-start.1 = (f32[2,512,256]{2,1,0:T(8,128)S(1)}, f32[2,512,256]{2,1,0:T(8,128)}, u32[]{:S(2)}, u32[]{:S(2)}) collective-permute-start(f32[2,512,256]{2,1,0:T(8,128)S(1)} %get-tuple-element.27.refs_1_.refs_3_), channel_id=1, source_target_pairs={{0,1},{1,0},{2,3},{3,2},{4,5},{5,4},{6,7},{7,6},{8,9},{9,8},{10,11... | collective-permute-start | bytes 3145736 | tf_op jit(solution)/shard_map/ppermute | solution.py:422
  6.3 7.6 %collective-permute-start = (f32[8,1024]{1,0:T(8,128)S(1)}, f32[8,1024]{1,0:T(8,128)S(1)}, u32[]{:S(2)}, u32[]{:S(2)}) collective-permute-start(f32[8,1024]{1,0:T(8,128)S(1)} %shard_map.83), channel_id=1, source_target_pairs={{0,4},{4,8},{8,12},{12,16},{16,20},{20,24},{24,28},{28,0},{1,5},{5... | collective-permute-start | bytes 98312 | tf_op jit(solution)/shard_map/ppermute | solution.py:464
  19.8 16.8 %collective-permute-start.6 = (f32[2,520,256]{2,1,0:T(8,128)}, f32[2,520,256]{2,1,0:T(8,128)}, u32[]{:S(2)}, u32[]{:S(2)}) collective-permute-start(f32[2,520,256]{2,1,0:T(8,128)} %get-tuple-element.34), channel_id=1, source_target_pairs={{0,1},{1,0},{2,3},{3,2},{4,5},{5,4},{6,7},{7,6},{8,9},{9,8},{10,11... | collective-permute-start | bytes 3194888 | tf_op jit(solution)/shard_map/ppermute | solution.py:422
  28.5 12.0 %collective-permute-start.7 = (f32[1,520,512]{2,1,0:T(8,128)}, f32[1,520,512]{2,1,0:T(8,128)}, u32[]{:S(2)}, u32[]{:S(2)}) collective-permute-start(f32[1,520,512]{2,1,0:T(8,128)} %get-tuple-element.36), channel_id=1, source_target_pairs={{0,1},{1,0},{2,3},{3,2},{4,5},{5,4},{6,7},{7,6},{8,9},{9,8},{10,11... | collective-permute-start | bytes 3194888 | tf_op jit(solution)/shard_map/ppermute | solution.py:422
  29.0 26.6 %collective-permute-start.2 = (f32[2,520,256]{2,1,0:T(8,128)}, f32[2,520,256]{2,1,0:T(8,128)}, u32[]{:S(2)}, u32[]{:S(2)}) collective-permute-start(f32[2,520,256]{2,1,0:T(8,128)} %get-tuple-element.31), channel_id=1, source_target_pairs={{0,1},{1,0},{2,3},{3,2},{4,5},{5,4},{6,7},{7,6},{8,9},{9,8},{10,11... | collective-permute-start | bytes 3194888 | tf_op jit(solution)/shard_map/ppermute | solution.py:422
  29.0 26.6 %collective-permute-start.5 = (f32[2,512,256]{2,1,0:T(8,128)}, f32[2,512,256]{2,1,0:T(8,128)}, u32[]{:S(2)}, u32[]{:S(2)}) collective-permute-start(f32[2,512,256]{2,1,0:T(8,128)} %add.12.refs_3_), channel_id=1, source_target_pairs={{0,2},{1,3},{2,0},{3,1},{4,6},{5,7},{6,4},{7,5},{8,10},{9,11},{10,... | collective-permute-start | bytes 3145736 | tf_op jit(solution)/shard_map/ppermute | solution.py:422
  30.5 33.7 %all-to-all-start.1 = ((f32[8,64,512]{2,1,0:T(8,128)}), f32[8,64,512]{2,1,0:T(8,128)S(1)}, u32[]{:S(2)}, u32[]{:S(2)}) async-start(f32[8,64,512]{2,1,0:T(8,128)} %shard_map.84.refs_2_), calls=%async_computation.1 | async-start | bytes 2097152 | tf_op jit(solution)/shard_map/all_to_all | solution.py:438
  34.9 1.2 collective-permute-start.3
  36.1 19.5 %collective-permute-start.4 = (f32[2,8,256]{2,1,0:T(8,128)S(1)}, f32[2,8,256]{2,1,0:T(8,128)S(1)}, u32[]{:S(2)}, u32[]{:S(2)}) collective-permute-start(f32[2,8,256]{2,1,0:T(8,128)S(1)} %add.13), channel_id=1, source_target_pairs={{0,2},{1,3},{2,0},{3,1},{4,6},{5,7},{6,4},{7,5},{8,10},{9,11},{10,... | collective-permute-start | bytes 49160 | tf_op jit(solution)/shard_map/ppermute | solution.py:422
  38.9 39.1 %collective-permute-start.9 = (f32[2,520,256]{2,1,0:T(8,128)}, f32[2,520,256]{2,1,0:T(8,128)}, u32[]{:S(2)}, u32[]{:S(2)}) collective-permute-start(f32[2,520,256]{2,1,0:T(8,128)} %add.14.refs_5_), channel_id=1, source_target_pairs={{0,2},{1,3},{2,0},{3,1},{4,6},{5,7},{6,4},{7,5},{8,10},{9,11},{10,... | collective-permute-start | bytes 3194888 | tf_op jit(solution)/shard_map/ppermute | solution.py:422
  64.2 13.8 %collective-permute-start.8 = (f32[2,520,256]{2,1,0:T(8,128)}, f32[2,520,256]{2,1,0:T(8,128)}, u32[]{:S(2)}, u32[]{:S(2)}) collective-permute-start(f32[2,520,256]{2,1,0:T(8,128)} %get-tuple-element.38), channel_id=1, source_target_pairs={{0,1},{1,0},{2,3},{3,2},{4,5},{5,4},{6,7},{7,6},{8,9},{9,8},{10,11... | collective-permute-start | bytes 3194888 | tf_op jit(solution)/shard_map/ppermute | solution.py:422
  80.1 22.2 %copy-start.4 = (f32[1,520,512]{2,1,0:T(8,128)S(1)}, f32[1,520,512]{2,1,0:T(8,128)}, u32[]{:S(2)}) copy-start(f32[1,520,512]{2,1,0:T(8,128)} %copy-done.3) | copy-start | bytes 3194884
  98.6 17.8 %all-to-all-start = ((f32[8,32,512]{2,1,0:T(8,128)}), f32[8,32,512]{2,1,0:T(8,128)S(1)}, u32[]{:S(2)}, u32[]{:S(2)}) async-start(f32[8,32,512]{2,1,0:T(8,128)} %shard_map.88.refs_3_), calls=%async_computation | async-start | bytes 1048576 | tf_op jit(solution)/shard_map/all_to_all | solution.py:438
  102.2 25.8 %collective-permute-start.18 = (f32[1,520,512]{2,1,0:T(8,128)S(1)}, f32[1,520,512]{2,1,0:T(8,128)}, u32[]{:S(2)}, u32[]{:S(2)}) collective-permute-start(f32[1,520,512]{2,1,0:T(8,128)S(1)} %copy-done.4), channel_id=1, source_target_pairs={{0,2},{1,3},{2,0},{3,1},{4,6},{5,7},{6,4},{7,5},{8,10},{9,11},{10,... | collective-permute-start | bytes 3194888 | tf_op jit(solution)/shard_map/ppermute | solution.py:422
  113.2 32.3 %collective-permute-start.17 = (f32[1,520,512]{2,1,0:T(8,128)}, f32[1,520,512]{2,1,0:T(8,128)S(1)}, u32[]{:S(2)}, u32[]{:S(2)}) collective-permute-start(f32[1,520,512]{2,1,0:T(8,128)} %get-tuple-element.48), channel_id=1, source_target_pairs={{0,1},{1,0},{2,3},{3,2},{4,5},{5,4},{6,7},{7,6},{8,9},{9,8},{10,11... | collective-permute-start | bytes 3194888 | tf_op jit(solution)/shard_map/ppermute | solution.py:422
  117.1 32.4 %all-to-all-start.3 = ((f32[8,32,512]{2,1,0:T(8,128)}), f32[8,32,512]{2,1,0:T(8,128)S(1)}, u32[]{:S(2)}, u32[]{:S(2)}) async-start(f32[8,32,512]{2,1,0:T(8,128)} %shard_map.94.refs_3_.refs_13_), calls=%async_computation.3 | async-start | bytes 1048576 | tf_op jit(solution)/shard_map/all_to_all | solution.py:438
  121.8 24.7 %copy-start.15 = (f32[1,520,512]{2,1,0:T(8,128)S(1)}, f32[1,520,512]{2,1,0:T(8,128)}, u32[]{:S(2)}) copy-start(f32[1,520,512]{2,1,0:T(8,128)} %copy-done.14) | copy-start | bytes 3194884
  124.4 6.5 %collective-permute-start.10 = (f32[32,512]{1,0:T(8,128)S(1)}, f32[32,512]{1,0:T(8,128)S(1)}, u32[]{:S(2)}, u32[]{:S(2)}) collective-permute-start(f32[32,512]{1,0:T(8,128)S(1)} %get-tuple-element.40), channel_id=1, source_target_pairs={{0,4},{4,0},{8,12},{12,8},{16,20},{20,16},{24,28},{28,24},{1,5},{5... | collective-permute-start | bytes 196616 | tf_op jit(solution)/shard_map/ppermute | solution.py:422
  126.5 6.6 %collective-permute-start.11 = (f32[32,512]{1,0:T(8,128)S(1)}, f32[32,512]{1,0:T(8,128)S(1)}, u32[]{:S(2)}, u32[]{:S(2)}) collective-permute-start(f32[32,512]{1,0:T(8,128)S(1)} %get-tuple-element.41), channel_id=1, source_target_pairs={{0,8},{4,12},{8,0},{12,4},{16,24},{20,28},{24,16},{28,20},{1,9},{5... | collective-permute-start | bytes 196616 | tf_op jit(solution)/shard_map/ppermute | solution.py:422
  128.0 7.8 %collective-permute-start.12 = (f32[32,512]{1,0:T(8,128)S(1)}, f32[32,512]{1,0:T(8,128)S(1)}, u32[]{:S(2)}, u32[]{:S(2)}) collective-permute-start(f32[32,512]{1,0:T(8,128)S(1)} %get-tuple-element.42), channel_id=1, source_target_pairs={{0,12},{4,8},{8,4},{12,0},{16,28},{20,24},{24,20},{28,16},{1,13},{... | collective-permute-start | bytes 196616 | tf_op jit(solution)/shard_map/ppermute | solution.py:422
  128.1 15.6 %collective-permute-start.13 = (f32[32,512]{1,0:T(8,128)S(1)}, f32[32,512]{1,0:T(8,128)S(1)}, u32[]{:S(2)}, u32[]{:S(2)}) collective-permute-start(f32[32,512]{1,0:T(8,128)S(1)} %get-tuple-element.43), channel_id=1, source_target_pairs={{0,16},{4,20},{8,24},{12,28},{16,0},{20,4},{24,8},{28,12},{1,17},{... | collective-permute-start | bytes 196616 | tf_op jit(solution)/shard_map/ppermute | solution.py:422
  130.9 14.6 %collective-permute-start.14 = (f32[32,512]{1,0:T(8,128)S(1)}, f32[32,512]{1,0:T(8,128)S(1)}, u32[]{:S(2)}, u32[]{:S(2)}) collective-permute-start(f32[32,512]{1,0:T(8,128)S(1)} %get-tuple-element.44), channel_id=1, source_target_pairs={{0,20},{4,16},{8,28},{12,24},{16,4},{20,0},{24,12},{28,8},{1,21},{... | collective-permute-start | bytes 196616 | tf_op jit(solution)/shard_map/ppermute | solution.py:422
  133.1 12.4 %collective-permute-start.15 = (f32[32,512]{1,0:T(8,128)S(1)}, f32[32,512]{1,0:T(8,128)S(1)}, u32[]{:S(2)}, u32[]{:S(2)}) collective-permute-start(f32[32,512]{1,0:T(8,128)S(1)} %get-tuple-element.45), channel_id=1, source_target_pairs={{0,24},{4,28},{8,16},{12,20},{16,8},{20,12},{24,0},{28,4},{1,25},{... | collective-permute-start | bytes 196616 | tf_op jit(solution)/shard_map/ppermute | solution.py:422
  135.8 9.7 %collective-permute-start.16 = (f32[32,512]{1,0:T(8,128)S(1)}, f32[32,512]{1,0:T(8,128)S(1)}, u32[]{:S(2)}, u32[]{:S(2)}) collective-permute-start(f32[32,512]{1,0:T(8,128)S(1)} %get-tuple-element.46), channel_id=1, source_target_pairs={{0,28},{4,24},{8,20},{12,16},{16,12},{20,8},{24,4},{28,0},{1,29},{... | collective-permute-start | bytes 196616 | tf_op jit(solution)/shard_map/ppermute | solution.py:422
  (24 other events, 113.5 us)
